TPU v7x, 256 devices: a whole 4x4x8 slice. The times are simulated.
256 devices in a mesh: depth: 8 (over x, y_lo), lat: 32 (over y_hi, z, core).
Axes of the slice: x: 4, y: 4 (y_hi: 2, y_lo: 2; y = y_hi * 2 + y_lo), z: 8, core: 2. Of those that a mesh axis runs over, the one named last changes fastest.
Arguments:
- probe: bfloat16 [2, 256, 256], replicated, may hold values from -6 to 6
- positions: int32 [2, 128, 2], P(None, 'lat'), may hold values from 0 to 255
- object_phase: bfloat16 [8, 8192, 512], P('depth', 'lat'), may hold values from -3.140625 to 3.140625
- propagator: float32 [256, 256], replicated, may hold values from -3.140625 to 3.140625
- stored: bfloat16 [8, 128, 2, 256, 256], P('depth', 'lat'), may hold values from -6 to 6
- measured: float32 [128, 256, 256], P('lat'), may hold values from 0 to 2
Outputs:
- leaving: bfloat16 [8, 128, 2, 256, 256], P('depth', 'lat')
- gradient: float32 [8, 2, 8192, 512], P('depth', None, 'lat')
Inputs may be any that keep to these rules, and one draw needn't show every extreme that they name: positions[d, q, 0] and positions[d, q, 1] are the row and column of the corner of probe q's window inside the tile of probe q; windows reach into the next tile's first rows.
All inputs are finite; a program needn't handle non-finite values.
Results may differ from a plain program's by a relative error of at most 0.04.
Values may be sent and summed in bfloat16 or wider, within the bound.
No kernel may reach another device: no remote copies, remote signals or barrier semaphores. Data moves between devices by JAX's collectives and lax.ppermute only.
A program may use at most 64 MiB of HBM per device.

v0:
```python
import math

import jax
import jax.numpy as jnp
from jax import lax
from jax.sharding import PartitionSpec as P


def from_behind(x, axis, by):
    devices = lax.axis_size(axis)
    return lax.ppermute(x, axis, [(i, (i + by) % devices) for i in range(devices)])


def shifted_2(block, axis, distance):
    devices = range(lax.axis_size(axis))
    route = [(i - distance, i) for i in devices if i - distance in devices]
    return lax.ppermute(block, axis, route)


def tables(npix):
    counter = jnp.arange(npix, dtype=jnp.int32)
    product = counter[:, None] * counter[None, :] % npix
    angles = 2.0 * math.pi / npix * product.astype(jnp.float32)
    factor = 1.0 / math.sqrt(npix)
    real_part = jnp.cos(angles) * factor
    imag_part = -jnp.sin(angles) * factor
    forward = jnp.stack(
        [jnp.stack([real_part, -imag_part]), jnp.stack([imag_part, real_part])]
    ).astype(jnp.bfloat16)
    inverse = jnp.stack(
        [jnp.stack([real_part, imag_part]), jnp.stack([-imag_part, real_part])]
    ).astype(jnp.bfloat16)
    return (forward, inverse)


def transform(table, wave):
    left = jnp.einsum("abjk,bkl->ajl", table, wave, preferred_element_type=jnp.float32).astype(
        jnp.bfloat16
    )
    return jnp.einsum("bjk,abkl->ajl", left, table, preferred_element_type=jnp.float32)


def times(first, second):
    first = first.astype(jnp.float32)
    real_part = first[0] * second[0] - first[1] * second[1]
    imag_part = first[0] * second[1] + first[1] * second[0]
    return jnp.stack([real_part, imag_part])


def conj_times(first, second):
    first = first.astype(jnp.float32)
    real_part = first[0] * second[0] + first[1] * second[1]
    imag_part = first[0] * second[1] - first[1] * second[0]
    return jnp.stack([real_part, imag_part])


def slice_forward(wave, transmit, kernel, forward, inverse):
    exited = times(wave, transmit).astype(jnp.bfloat16)
    spectrum = transform(forward, exited)
    shifted = times(kernel, spectrum).astype(jnp.bfloat16)
    return transform(inverse, shifted).astype(jnp.bfloat16)


def slice_adjoint(adjoint, wave, transmit, kernel, forward, inverse):
    spectrum = transform(forward, adjoint)
    shifted = conj_times(kernel, spectrum).astype(jnp.bfloat16)
    exited = transform(inverse, shifted)
    term = conj_times(wave, exited)
    return (conj_times(transmit, exited).astype(jnp.bfloat16), term)


def far_adjoint(exit_wave, intensity, forward, inverse):
    field = transform(forward, exit_wave)
    power = field[0] * field[0] + field[1] * field[1]
    weight = (power - intensity)[None] * field
    return transform(inverse, weight.astype(jnp.bfloat16)).astype(jnp.bfloat16)


def body(probe, positions, object_phase, propagator, stored, measured):
    npix = probe.shape[-1]
    slices, tile_rows, columns = object_phase.shape
    probes = positions.shape[1]
    depth_size = lax.axis_size("depth")
    segment = lax.axis_index("depth")
    forward, inverse = tables(npix)
    kernel = jnp.stack([jnp.cos(propagator), jnp.sin(propagator)])
    edge = from_behind(object_phase, "lat", -1)
    extended = jnp.concatenate([object_phase, edge], axis=1).astype(jnp.float32)
    transmit = jnp.stack([jnp.cos(extended), jnp.sin(extended)], axis=1)
    empty_wave = jnp.zeros((2, npix, npix), jnp.bfloat16)
    blank_piece = jnp.zeros((slices, 2, npix, npix), jnp.float32)

    def cut(row, col):
        return lax.dynamic_slice(transmit, (0, 0, row, col), (slices, 2, npix, npix))

    def advance(moment, carry):
        ahead_in, behind_in, leaving, gradient = carry
        ahead_index = moment - segment
        ahead_live = (ahead_index >= 0) & (ahead_index < probes)
        ahead_slot = jnp.clip(ahead_index, 0, probes - 1)
        ahead_row = positions[0, ahead_slot, 0]
        ahead_col = positions[0, ahead_slot, 1]
        entering = jnp.where(segment == 0, probe, ahead_in)

        def run_ahead():
            window = cut(ahead_row, ahead_col)
            wave = entering
            wave = slice_forward(wave, window[0], kernel, forward, inverse)
            return wave

        ahead_out = lax.cond(ahead_live, run_ahead, lambda: empty_wave)
        kept = jnp.where(ahead_live, ahead_out, leaving[ahead_slot])
        leaving = lax.dynamic_update_index_in_dim(leaving, kept, ahead_slot, 0)
        behind_index = moment - (depth_size - 1 - segment)
        behind_live = (behind_index >= 0) & (behind_index < probes)
        behind_slot = jnp.clip(behind_index, 0, probes - 1)
        behind_row = positions[1, behind_slot, 0]
        behind_col = positions[1, behind_slot, 1]

        def run_behind():
            window = cut(behind_row, behind_col)
            wave = stored[0, behind_slot]
            index = 0
            inputs = [wave]
            wave = slice_forward(wave, window[index], kernel, forward, inverse)
            final_wave = wave
            adjoint = lax.cond(
                segment == depth_size - 1,
                lambda: far_adjoint(final_wave, measured[behind_slot], forward, inverse),
                lambda: behind_in,
            )
            terms = [None] * slices
            for index in reversed(range(slices)):
                adjoint, terms[index] = slice_adjoint(
                    adjoint, inputs[index], window[index], kernel, forward, inverse
                )
            corner = (0, 0, behind_row, behind_col)
            summed = lax.dynamic_slice(gradient, corner, blank_piece.shape) + jnp.stack(terms)
            return (adjoint, lax.dynamic_update_slice(gradient, summed, corner))

        behind_out, gradient = lax.cond(behind_live, run_behind, lambda: (empty_wave, gradient))
        ahead_next = shifted_2(ahead_out, "depth", 1)
        behind_next = shifted_2(behind_out, "depth", -1)
        return (ahead_next, behind_next, leaving, gradient)

    ticks = probes + depth_size - 1
    initial = (
        empty_wave,
        empty_wave,
        jnp.zeros((probes, 2, npix, npix), jnp.bfloat16),
        jnp.zeros((slices, 2, tile_rows + npix, columns), jnp.float32),
    )
    _, _, leaving, gradient = lax.fori_loop(0, ticks, advance, initial)
    rim_terms = from_behind(gradient[:, :, tile_rows:].astype(jnp.bfloat16), "lat", 1).astype(
        jnp.float32
    )
    result = gradient[:, :, :tile_rows].at[:, :, :npix].add(rim_terms)
    return (leaving[None], result)


def solution(mesh):
    return jax.shard_map(
        body,
        mesh=mesh,
        in_specs=(
            P(),
            P(None, "lat", None),
            P("depth", "lat", None),
            P(),
            P("depth", "lat", None, None, None),
            P("lat", None, None),
        ),
        out_specs=(P("depth", "lat", None, None, None), P("depth", None, "lat", None)),
        check_vma=False,
    )
```

profile of v0, /device:TPU:16, one launch (start us, length us, event | category | flops | bytes accessed | tf_op | source)
XLA Modules:
  0.0 427.2 jit_solution(12944001682942653103)
XLA Ops:
  0.6 5.1 %collective-permute-start.2 = (bf16[1,256,512]{2,1,0:T(8,128)(2,1)}, bf16[1,256,512]{2,1,0:T(8,128)(2,1)S(1)}, u32[]{:S(2)}, u32[]{:S(2)}) collective-permute-start(bf16[1,256,512]{2,1,0:T(8,128)(2,1)} %param.20), channel_id=1, source_target_pairs={{0,31},{1,0},{2,1},{3,2},{4,3},{5,4},{6,5},{7,6},{8,7},{9,8},{10,9... | collective-permute-start | bytes 786440 | tf_op jit(solution)/shard_map/ppermute | solution.py:11
  10.2 3.7 convert_cosine_fusion
  13.8 1.5 pad_maximum_fusion.1
  17.1 1.6 broadcast_in_dim.32
  18.7 392.6 %while.28 = (s32[]{:T(128)}, bf16[2,256,256]{2,1,0:T(8,128)(2,1)}, bf16[2,256,256]{2,1,0:T(8,128)(2,1)S(1)}, bf16[4,2,256,256]{3,2,1,0:T(8,128)(2,1)}, f32[1,2,5...) while((s32[]{:T(128)}, bf16[2,256,256]{2,1,0:T(8,128)(2,1)}, ...), condition=%wide.region_7.8_spmd, body=%wide.region_0.7_spmd.sunk | while | flops 2156527616 | bytes 30148020 | solution.py:153
  18.7 8.3 %conditional.5 = (bf16[2,256,256]{2,1,0:T(8,128)(2,1)S(1)}) conditional(s32[]{:T(128)} %convert_element_type.241, () %tuple.94, (pred[]{:T(512)}, bf16[2,256,256]{2,1,0:T(8,128)(2,1)}, bf16[2,256,256]{2,1,0:T(8,128)(2,1)}, s32[2,4,2]{1,2,0:T(2,128)S(1)}, s32[]{:T(128)}, /*index=5*/f32[1,2,512,512]{3,2,1,0:T(8,128)}, ...), branch_computations={%region_1.1_spmd, %region_2.2_spmd} | conditional | flops 539623424 | bytes 6029433 | solution.py:111
  27.0 2.0 collective-permute-start
  32.8 2.5 collective-permute-done
  35.3 3.0 collective-permute-done.1
  38.2 8.3 %conditional.5 = (bf16[2,256,256]{2,1,0:T(8,128)(2,1)S(1)}) conditional(s32[]{:T(128)} %convert_element_type.241, () %tuple.94, (pred[]{:T(512)}, bf16[2,256,256]{2,1,0:T(8,128)(2,1)}, bf16[2,256,256]{2,1,0:T(8,128)(2,1)}, s32[2,4,2]{1,2,0:T(2,128)S(1)}, s32[]{:T(128)}, /*index=5*/f32[1,2,512,512]{3,2,1,0:T(8,128)}, ...), branch_computations={%region_1.1_spmd, %region_2.2_spmd} | conditional | flops 539623424 | bytes 6029433 | solution.py:111
  46.5 2.3 collective-permute-start
  52.6 5.3 %collective-permute-done = bf16[2,256,256]{2,1,0:T(8,128)(2,1)} collective-permute-done((bf16[2,256,256]{2,1,0:T(8,128)(2,1)S(1)}, bf16[2,256,256]{2,1,0:T(8,128)(2,1)}, u32[]{:S(2)}, u32[]{:S(2)}) %collective-permute-start) | collective-permute-done | bytes 262176 | tf_op jit(solution)/shard_map/while/body/eval_jaxpr/ppermute | solution.py:17
  58.0 8.3 %conditional.5 = (bf16[2,256,256]{2,1,0:T(8,128)(2,1)S(1)}) conditional(s32[]{:T(128)} %convert_element_type.241, () %tuple.94, (pred[]{:T(512)}, bf16[2,256,256]{2,1,0:T(8,128)(2,1)}, bf16[2,256,256]{2,1,0:T(8,128)(2,1)}, s32[2,4,2]{1,2,0:T(2,128)S(1)}, s32[]{:T(128)}, /*index=5*/f32[1,2,512,512]{3,2,1,0:T(8,128)}, ...), branch_computations={%region_1.1_spmd, %region_2.2_spmd} | conditional | flops 539623424 | bytes 6029433 | solution.py:111
  66.3 5.1 %collective-permute-start = (bf16[2,256,256]{2,1,0:T(8,128)(2,1)S(1)}, bf16[2,256,256]{2,1,0:T(8,128)(2,1)}, u32[]{:S(2)}, u32[]{:S(2)}) collective-permute-start(bf16[2,256,256]{2,1,0:T(8,128)(2,1)S(1)} %get-tuple-element.764), channel_id=1, source_target_pairs={{0,32},{32,64},{64,96},{96,128},{128,160},{160,192},{192,224},{1,3... | collective-permute-start | bytes 786440 | tf_op jit(solution)/shard_map/while/body/eval_jaxpr/ppermute | solution.py:17
  75.1 3.5 collective-permute-done
  78.7 1.9 collective-permute-done.1
  80.6 8.3 %conditional.5 = (bf16[2,256,256]{2,1,0:T(8,128)(2,1)S(1)}) conditional(s32[]{:T(128)} %convert_element_type.241, () %tuple.94, (pred[]{:T(512)}, bf16[2,256,256]{2,1,0:T(8,128)(2,1)}, bf16[2,256,256]{2,1,0:T(8,128)(2,1)}, s32[2,4,2]{1,2,0:T(2,128)S(1)}, s32[]{:T(128)}, /*index=5*/f32[1,2,512,512]{3,2,1,0:T(8,128)}, ...), branch_computations={%region_1.1_spmd, %region_2.2_spmd} | conditional | flops 539623424 | bytes 6029433 | solution.py:111
  88.9 3.3 collective-permute-start
  95.9 5.4 %collective-permute-done.1 = bf16[2,256,256]{2,1,0:T(8,128)(2,1)S(1)} collective-permute-done((bf16[2,256,256]{2,1,0:T(8,128)(2,1)}, bf16[2,256,256]{2,1,0:T(8,128)(2,1)S(1)}, u32[]{:S(2)}, u32[]{:S(2)}) %collective-permute-start.1) | collective-permute-done | bytes 262176 | tf_op jit(solution)/shard_map/while/body/eval_jaxpr/ppermute | solution.py:17
  101.4 23.3 %collective-permute-start = (bf16[2,256,256]{2,1,0:T(8,128)(2,1)S(1)}, bf16[2,256,256]{2,1,0:T(8,128)(2,1)}, u32[]{:S(2)}, u32[]{:S(2)}) collective-permute-start(bf16[2,256,256]{2,1,0:T(8,128)(2,1)S(1)} %get-tuple-element.764), channel_id=1, source_target_pairs={{0,32},{32,64},{64,96},{96,128},{128,160},{160,192},{192,224},{1,3... | collective-permute-start | bytes 786440 | tf_op jit(solution)/shard_map/while/body/eval_jaxpr/ppermute | solution.py:17
  128.5 18.5 %collective-permute-done.1 = bf16[2,256,256]{2,1,0:T(8,128)(2,1)S(1)} collective-permute-done((bf16[2,256,256]{2,1,0:T(8,128)(2,1)}, bf16[2,256,256]{2,1,0:T(8,128)(2,1)S(1)}, u32[]{:S(2)}, u32[]{:S(2)}) %collective-permute-start.1) | collective-permute-done | bytes 262176 | tf_op jit(solution)/shard_map/while/body/eval_jaxpr/ppermute | solution.py:17
  147.1 24.3 %collective-permute-start = (bf16[2,256,256]{2,1,0:T(8,128)(2,1)S(1)}, bf16[2,256,256]{2,1,0:T(8,128)(2,1)}, u32[]{:S(2)}, u32[]{:S(2)}) collective-permute-start(bf16[2,256,256]{2,1,0:T(8,128)(2,1)S(1)} %get-tuple-element.764), channel_id=1, source_target_pairs={{0,32},{32,64},{64,96},{96,128},{128,160},{160,192},{192,224},{1,3... | collective-permute-start | bytes 786440 | tf_op jit(solution)/shard_map/while/body/eval_jaxpr/ppermute | solution.py:17
  175.2 34.9 %collective-permute-done.1 = bf16[2,256,256]{2,1,0:T(8,128)(2,1)S(1)} collective-permute-done((bf16[2,256,256]{2,1,0:T(8,128)(2,1)}, bf16[2,256,256]{2,1,0:T(8,128)(2,1)S(1)}, u32[]{:S(2)}, u32[]{:S(2)}) %collective-permute-start.1) | collective-permute-done | bytes 262176 | tf_op jit(solution)/shard_map/while/body/eval_jaxpr/ppermute | solution.py:17
  210.1 21.9 %collective-permute-start = (bf16[2,256,256]{2,1,0:T(8,128)(2,1)S(1)}, bf16[2,256,256]{2,1,0:T(8,128)(2,1)}, u32[]{:S(2)}, u32[]{:S(2)}) collective-permute-start(bf16[2,256,256]{2,1,0:T(8,128)(2,1)S(1)} %get-tuple-element.764), channel_id=1, source_target_pairs={{0,32},{32,64},{64,96},{96,128},{128,160},{160,192},{192,224},{1,3... | collective-permute-start | bytes 786440 | tf_op jit(solution)/shard_map/while/body/eval_jaxpr/ppermute | solution.py:17
  235.8 23.8 %collective-permute-done.1 = bf16[2,256,256]{2,1,0:T(8,128)(2,1)S(1)} collective-permute-done((bf16[2,256,256]{2,1,0:T(8,128)(2,1)}, bf16[2,256,256]{2,1,0:T(8,128)(2,1)S(1)}, u32[]{:S(2)}, u32[]{:S(2)}) %collective-permute-start.1) | collective-permute-done | bytes 262176 | tf_op jit(solution)/shard_map/while/body/eval_jaxpr/ppermute | solution.py:17
  259.6 10.7 %collective-permute-start = (bf16[2,256,256]{2,1,0:T(8,128)(2,1)S(1)}, bf16[2,256,256]{2,1,0:T(8,128)(2,1)}, u32[]{:S(2)}, u32[]{:S(2)}) collective-permute-start(bf16[2,256,256]{2,1,0:T(8,128)(2,1)S(1)} %get-tuple-element.764), channel_id=1, source_target_pairs={{0,32},{32,64},{64,96},{96,128},{128,160},{160,192},{192,224},{1,3... | collective-permute-start | bytes 786440 | tf_op jit(solution)/shard_map/while/body/eval_jaxpr/ppermute | solution.py:17
  270.3 19.8 %conditional.6 = (bf16[2,256,256]{2,1,0:T(8,128)(2,1)}, f32[1,2,512,512]{3,2,1,0:T(8,128)}) conditional(s32[]{:T(128)} %convert_element_type.242, f32[1,2,512,512]{3,2,1,0:T(8,128)} %get-tuple-element.725, (s32[]{:T(128)}, s32[2,4,2]{1,2,0:T(2,128)S(1)}, f32[1,2,512,512]{3,2,1,0:T(8,128)}, s32[]{:T(128)}, bf16[1,4,2,256,256]{4,3,2,1,0:T(8,128)(2,1)}, ...), branch_computations={%region_3.3_spmd, %region_4.6_spmd} | conditional | flops 1616773120 | bytes 20709656 | solution.py:141
  279.9 1.4 multiply_add_fusion
  281.3 1.4 fusion.44
  283.4 6.7 %dynamic_update_slice.11 = f32[1,2,512,512]{3,2,1,0:T(8,128)} dynamic-update-slice(f32[1,2,512,512]{3,2,1,0:T(8,128)} %get-tuple-element.496, f32[1,2,256,256]{3,2,1,0:T(8,128)S(1)} %fusion.44, s32[]{:T(128)} %constant.127.clone, s32[]{:T(128)} %constant.127.clone, s32[]{:T(128)S(6)} %select_n.99, s32[]{:T(128)S(6)} %select_n.100) | dynamic-update-slice | bytes 1048580 | tf_op jit(solution)/shard_map/while/body/eval_jaxpr/cond/branch_1_fun/dynamic_update_slice | solution.py:139
  293.2 5.4 %collective-permute-done.1 = bf16[2,256,256]{2,1,0:T(8,128)(2,1)S(1)} collective-permute-done((bf16[2,256,256]{2,1,0:T(8,128)(2,1)}, bf16[2,256,256]{2,1,0:T(8,128)(2,1)S(1)}, u32[]{:S(2)}, u32[]{:S(2)}) %collective-permute-start.1) | collective-permute-done | bytes 262176 | tf_op jit(solution)/shard_map/while/body/eval_jaxpr/ppermute | solution.py:17
  298.6 4.3 collective-permute-start
  302.9 19.2 %conditional.6 = (bf16[2,256,256]{2,1,0:T(8,128)(2,1)}, f32[1,2,512,512]{3,2,1,0:T(8,128)}) conditional(s32[]{:T(128)} %convert_element_type.242, f32[1,2,512,512]{3,2,1,0:T(8,128)} %get-tuple-element.725, (s32[]{:T(128)}, s32[2,4,2]{1,2,0:T(2,128)S(1)}, f32[1,2,512,512]{3,2,1,0:T(8,128)}, s32[]{:T(128)}, bf16[1,4,2,256,256]{4,3,2,1,0:T(8,128)(2,1)}, ...), branch_computations={%region_3.3_spmd, %region_4.6_spmd} | conditional | flops 1616773120 | bytes 20709656 | solution.py:141
  313.9 1.4 fusion.44
  316.0 6.1 %dynamic_update_slice.11 = f32[1,2,512,512]{3,2,1,0:T(8,128)} dynamic-update-slice(f32[1,2,512,512]{3,2,1,0:T(8,128)} %get-tuple-element.496, f32[1,2,256,256]{3,2,1,0:T(8,128)S(1)} %fusion.44, s32[]{:T(128)} %constant.127.clone, s32[]{:T(128)} %constant.127.clone, s32[]{:T(128)S(6)} %select_n.99, s32[]{:T(128)S(6)} %select_n.100) | dynamic-update-slice | bytes 1048580 | tf_op jit(solution)/shard_map/while/body/eval_jaxpr/cond/branch_1_fun/dynamic_update_slice | solution.py:139
  325.1 13.2 %collective-permute-done.1 = bf16[2,256,256]{2,1,0:T(8,128)(2,1)S(1)} collective-permute-done((bf16[2,256,256]{2,1,0:T(8,128)(2,1)}, bf16[2,256,256]{2,1,0:T(8,128)(2,1)S(1)}, u32[]{:S(2)}, u32[]{:S(2)}) %collective-permute-start.1) | collective-permute-done | bytes 262176 | tf_op jit(solution)/shard_map/while/body/eval_jaxpr/ppermute | solution.py:17
  338.4 6.4 %collective-permute-start = (bf16[2,256,256]{2,1,0:T(8,128)(2,1)S(1)}, bf16[2,256,256]{2,1,0:T(8,128)(2,1)}, u32[]{:S(2)}, u32[]{:S(2)}) collective-permute-start(bf16[2,256,256]{2,1,0:T(8,128)(2,1)S(1)} %get-tuple-element.764), channel_id=1, source_target_pairs={{0,32},{32,64},{64,96},{96,128},{128,160},{160,192},{192,224},{1,3... | collective-permute-start | bytes 786440 | tf_op jit(solution)/shard_map/while/body/eval_jaxpr/ppermute | solution.py:17
  344.8 18.9 %conditional.6 = (bf16[2,256,256]{2,1,0:T(8,128)(2,1)}, f32[1,2,512,512]{3,2,1,0:T(8,128)}) conditional(s32[]{:T(128)} %convert_element_type.242, f32[1,2,512,512]{3,2,1,0:T(8,128)} %get-tuple-element.725, (s32[]{:T(128)}, s32[2,4,2]{1,2,0:T(2,128)S(1)}, f32[1,2,512,512]{3,2,1,0:T(8,128)}, s32[]{:T(128)}, bf16[1,4,2,256,256]{4,3,2,1,0:T(8,128)(2,1)}, ...), branch_computations={%region_3.3_spmd, %region_4.6_spmd} | conditional | flops 1616773120 | bytes 20709656 | solution.py:141
  355.8 1.4 fusion.44
  357.9 5.8 %dynamic_update_slice.11 = f32[1,2,512,512]{3,2,1,0:T(8,128)} dynamic-update-slice(f32[1,2,512,512]{3,2,1,0:T(8,128)} %get-tuple-element.496, f32[1,2,256,256]{3,2,1,0:T(8,128)S(1)} %fusion.44, s32[]{:T(128)} %constant.127.clone, s32[]{:T(128)} %constant.127.clone, s32[]{:T(128)S(6)} %select_n.99, s32[]{:T(128)S(6)} %select_n.100) | dynamic-update-slice | bytes 1048580 | tf_op jit(solution)/shard_map/while/body/eval_jaxpr/cond/branch_1_fun/dynamic_update_slice | solution.py:139
  366.7 5.6 %collective-permute-done.1 = bf16[2,256,256]{2,1,0:T(8,128)(2,1)S(1)} collective-permute-done((bf16[2,256,256]{2,1,0:T(8,128)(2,1)}, bf16[2,256,256]{2,1,0:T(8,128)(2,1)S(1)}, u32[]{:S(2)}, u32[]{:S(2)}) %collective-permute-start.1) | collective-permute-done | bytes 262176 | tf_op jit(solution)/shard_map/while/body/eval_jaxpr/ppermute | solution.py:17
  372.4 5.5 %collective-permute-start = (bf16[2,256,256]{2,1,0:T(8,128)(2,1)S(1)}, bf16[2,256,256]{2,1,0:T(8,128)(2,1)}, u32[]{:S(2)}, u32[]{:S(2)}) collective-permute-start(bf16[2,256,256]{2,1,0:T(8,128)(2,1)S(1)} %get-tuple-element.764), channel_id=1, source_target_pairs={{0,32},{32,64},{64,96},{96,128},{128,160},{160,192},{192,224},{1,3... | collective-permute-start | bytes 786440 | tf_op jit(solution)/shard_map/while/body/eval_jaxpr/ppermute | solution.py:17
  378.0 19.8 %conditional.6 = (bf16[2,256,256]{2,1,0:T(8,128)(2,1)}, f32[1,2,512,512]{3,2,1,0:T(8,128)}) conditional(s32[]{:T(128)} %convert_element_type.242, f32[1,2,512,512]{3,2,1,0:T(8,128)} %get-tuple-element.725, (s32[]{:T(128)}, s32[2,4,2]{1,2,0:T(2,128)S(1)}, f32[1,2,512,512]{3,2,1,0:T(8,128)}, s32[]{:T(128)}, bf16[1,4,2,256,256]{4,3,2,1,0:T(8,128)(2,1)}, ...), branch_computations={%region_3.3_spmd, %region_4.6_spmd} | conditional | flops 1616773120 | bytes 20709656 | solution.py:141
  388.9 1.4 fusion.44
  391.0 6.7 %dynamic_update_slice.11 = f32[1,2,512,512]{3,2,1,0:T(8,128)} dynamic-update-slice(f32[1,2,512,512]{3,2,1,0:T(8,128)} %get-tuple-element.496, f32[1,2,256,256]{3,2,1,0:T(8,128)S(1)} %fusion.44, s32[]{:T(128)} %constant.127.clone, s32[]{:T(128)} %constant.127.clone, s32[]{:T(128)S(6)} %select_n.99, s32[]{:T(128)S(6)} %select_n.100) | dynamic-update-slice | bytes 1048580 | tf_op jit(solution)/shard_map/while/body/eval_jaxpr/cond/branch_1_fun/dynamic_update_slice | solution.py:139
  400.8 10.5 %collective-permute-done.1 = bf16[2,256,256]{2,1,0:T(8,128)(2,1)S(1)} collective-permute-done((bf16[2,256,256]{2,1,0:T(8,128)(2,1)}, bf16[2,256,256]{2,1,0:T(8,128)(2,1)S(1)}, u32[]{:S(2)}, u32[]{:S(2)}) %collective-permute-start.1) | collective-permute-done | bytes 262176 | tf_op jit(solution)/shard_map/while/body/eval_jaxpr/ppermute | solution.py:17
  412.7 12.2 %collective-permute-done.3 = bf16[1,2,256,512]{3,2,1,0:T(8,128)(2,1)S(1)} collective-permute-done((bf16[1,2,256,512]{3,2,1,0:T(8,128)(2,1)S(1)}, bf16[1,2,256,512]{3,2,1,0:T(8,128)(2,1)S(1)}, u32[]{:S(2)}, u32[]{:S(2)}) %collective-permute-start.3) | collective-permute-done | bytes 524320 | tf_op jit(solution)/shard_map/ppermute | solution.py:11
  424.9 2.4 convert_add_fusion
  (167 shorter events, 100.8 us)
Async XLA Ops:
  0.6 8.3 %copy-start = (f32[256,256]{1,0:T(8,128)S(1)}, f32[256,256]{1,0:T(8,128)}, u32[]{:S(2)}) copy-start(f32[256,256]{1,0:T(8,128)} %param.21) | copy-start | bytes 786436
  0.6 9.5 %collective-permute-start.2 = (bf16[1,256,512]{2,1,0:T(8,128)(2,1)}, bf16[1,256,512]{2,1,0:T(8,128)(2,1)S(1)}, u32[]{:S(2)}, u32[]{:S(2)}) collective-permute-start(bf16[1,256,512]{2,1,0:T(8,128)(2,1)} %param.20), channel_id=1, source_target_pairs={{0,31},{1,0},{2,1},{3,2},{4,3},{5,4},{6,5},{7,6},{8,7},{9,8},{10,9... | collective-permute-start | bytes 786440 | tf_op jit(solution)/shard_map/ppermute | solution.py:11
  8.8 1.4 copy-start.1
  15.3 3.4 copy-start.2
  27.0 8.2 %collective-permute-start = (bf16[2,256,256]{2,1,0:T(8,128)(2,1)S(1)}, bf16[2,256,256]{2,1,0:T(8,128)(2,1)}, u32[]{:S(2)}, u32[]{:S(2)}) collective-permute-start(bf16[2,256,256]{2,1,0:T(8,128)(2,1)S(1)} %get-tuple-element.764), channel_id=1, source_target_pairs={{0,32},{32,64},{64,96},{96,128},{128,160},{160,192},{192,224},{1,3... | collective-permute-start | bytes 786440 | tf_op jit(solution)/shard_map/while/body/eval_jaxpr/ppermute | solution.py:17
  29.8 8.5 %collective-permute-start.1 = (bf16[2,256,256]{2,1,0:T(8,128)(2,1)}, bf16[2,256,256]{2,1,0:T(8,128)(2,1)S(1)}, u32[]{:S(2)}, u32[]{:S(2)}) collective-permute-start(bf16[2,256,256]{2,1,0:T(8,128)(2,1)} %get-tuple-element.694), channel_id=1, source_target_pairs={{32,0},{64,32},{96,64},{128,96},{160,128},{192,160},{224,192},{33,... | collective-permute-start | bytes 786440 | tf_op jit(solution)/shard_map/while/body/eval_jaxpr/ppermute | solution.py:17
  46.5 11.3 %collective-permute-start = (bf16[2,256,256]{2,1,0:T(8,128)(2,1)S(1)}, bf16[2,256,256]{2,1,0:T(8,128)(2,1)}, u32[]{:S(2)}, u32[]{:S(2)}) collective-permute-start(bf16[2,256,256]{2,1,0:T(8,128)(2,1)S(1)} %get-tuple-element.764), channel_id=1, source_target_pairs={{0,32},{32,64},{64,96},{96,128},{128,160},{160,192},{192,224},{1,3... | collective-permute-start | bytes 786440 | tf_op jit(solution)/shard_map/while/body/eval_jaxpr/ppermute | solution.py:17
  49.6 8.5 %collective-permute-start.1 = (bf16[2,256,256]{2,1,0:T(8,128)(2,1)}, bf16[2,256,256]{2,1,0:T(8,128)(2,1)S(1)}, u32[]{:S(2)}, u32[]{:S(2)}) collective-permute-start(bf16[2,256,256]{2,1,0:T(8,128)(2,1)} %get-tuple-element.694), channel_id=1, source_target_pairs={{32,0},{64,32},{96,64},{128,96},{160,128},{192,160},{224,192},{33,... | collective-permute-start | bytes 786440 | tf_op jit(solution)/shard_map/while/body/eval_jaxpr/ppermute | solution.py:17
  66.3 12.3 %collective-permute-start = (bf16[2,256,256]{2,1,0:T(8,128)(2,1)S(1)}, bf16[2,256,256]{2,1,0:T(8,128)(2,1)}, u32[]{:S(2)}, u32[]{:S(2)}) collective-permute-start(bf16[2,256,256]{2,1,0:T(8,128)(2,1)S(1)} %get-tuple-element.764), channel_id=1, source_target_pairs={{0,32},{32,64},{64,96},{96,128},{128,160},{160,192},{192,224},{1,3... | collective-permute-start | bytes 786440 | tf_op jit(solution)/shard_map/while/body/eval_jaxpr/ppermute | solution.py:17
  72.1 8.5 %collective-permute-start.1 = (bf16[2,256,256]{2,1,0:T(8,128)(2,1)}, bf16[2,256,256]{2,1,0:T(8,128)(2,1)S(1)}, u32[]{:S(2)}, u32[]{:S(2)}) collective-permute-start(bf16[2,256,256]{2,1,0:T(8,128)(2,1)} %get-tuple-element.694), channel_id=1, source_target_pairs={{32,0},{64,32},{96,64},{128,96},{160,128},{192,160},{224,192},{33,... | collective-permute-start | bytes 786440 | tf_op jit(solution)/shard_map/while/body/eval_jaxpr/ppermute | solution.py:17
  88.9 7.1 %collective-permute-start = (bf16[2,256,256]{2,1,0:T(8,128)(2,1)S(1)}, bf16[2,256,256]{2,1,0:T(8,128)(2,1)}, u32[]{:S(2)}, u32[]{:S(2)}) collective-permute-start(bf16[2,256,256]{2,1,0:T(8,128)(2,1)S(1)} %get-tuple-element.764), channel_id=1, source_target_pairs={{0,32},{32,64},{64,96},{96,128},{128,160},{160,192},{192,224},{1,3... | collective-permute-start | bytes 786440 | tf_op jit(solution)/shard_map/while/body/eval_jaxpr/ppermute | solution.py:17
  92.9 8.5 %collective-permute-start.1 = (bf16[2,256,256]{2,1,0:T(8,128)(2,1)}, bf16[2,256,256]{2,1,0:T(8,128)(2,1)S(1)}, u32[]{:S(2)}, u32[]{:S(2)}) collective-permute-start(bf16[2,256,256]{2,1,0:T(8,128)(2,1)} %get-tuple-element.694), channel_id=1, source_target_pairs={{32,0},{64,32},{96,64},{128,96},{160,128},{192,160},{224,192},{33,... | collective-permute-start | bytes 786440 | tf_op jit(solution)/shard_map/while/body/eval_jaxpr/ppermute | solution.py:17
  101.4 27.1 %collective-permute-start = (bf16[2,256,256]{2,1,0:T(8,128)(2,1)S(1)}, bf16[2,256,256]{2,1,0:T(8,128)(2,1)}, u32[]{:S(2)}, u32[]{:S(2)}) collective-permute-start(bf16[2,256,256]{2,1,0:T(8,128)(2,1)S(1)} %get-tuple-element.764), channel_id=1, source_target_pairs={{0,32},{32,64},{64,96},{96,128},{128,160},{160,192},{192,224},{1,3... | collective-permute-start | bytes 786440 | tf_op jit(solution)/shard_map/while/body/eval_jaxpr/ppermute | solution.py:17
  125.5 21.6 %collective-permute-start.1 = (bf16[2,256,256]{2,1,0:T(8,128)(2,1)}, bf16[2,256,256]{2,1,0:T(8,128)(2,1)S(1)}, u32[]{:S(2)}, u32[]{:S(2)}) collective-permute-start(bf16[2,256,256]{2,1,0:T(8,128)(2,1)} %get-tuple-element.694), channel_id=1, source_target_pairs={{32,0},{64,32},{96,64},{128,96},{160,128},{192,160},{224,192},{33,... | collective-permute-start | bytes 786440 | tf_op jit(solution)/shard_map/while/body/eval_jaxpr/ppermute | solution.py:17
  147.1 28.1 %collective-permute-start = (bf16[2,256,256]{2,1,0:T(8,128)(2,1)S(1)}, bf16[2,256,256]{2,1,0:T(8,128)(2,1)}, u32[]{:S(2)}, u32[]{:S(2)}) collective-permute-start(bf16[2,256,256]{2,1,0:T(8,128)(2,1)S(1)} %get-tuple-element.764), channel_id=1, source_target_pairs={{0,32},{32,64},{64,96},{96,128},{128,160},{160,192},{192,224},{1,3... | collective-permute-start | bytes 786440 | tf_op jit(solution)/shard_map/while/body/eval_jaxpr/ppermute | solution.py:17
  172.1 38.0 %collective-permute-start.1 = (bf16[2,256,256]{2,1,0:T(8,128)(2,1)}, bf16[2,256,256]{2,1,0:T(8,128)(2,1)S(1)}, u32[]{:S(2)}, u32[]{:S(2)}) collective-permute-start(bf16[2,256,256]{2,1,0:T(8,128)(2,1)} %get-tuple-element.694), channel_id=1, source_target_pairs={{32,0},{64,32},{96,64},{128,96},{160,128},{192,160},{224,192},{33,... | collective-permute-start | bytes 786440 | tf_op jit(solution)/shard_map/while/body/eval_jaxpr/ppermute | solution.py:17
  210.1 25.7 %collective-permute-start = (bf16[2,256,256]{2,1,0:T(8,128)(2,1)S(1)}, bf16[2,256,256]{2,1,0:T(8,128)(2,1)}, u32[]{:S(2)}, u32[]{:S(2)}) collective-permute-start(bf16[2,256,256]{2,1,0:T(8,128)(2,1)S(1)} %get-tuple-element.764), channel_id=1, source_target_pairs={{0,32},{32,64},{64,96},{96,128},{128,160},{160,192},{192,224},{1,3... | collective-permute-start | bytes 786440 | tf_op jit(solution)/shard_map/while/body/eval_jaxpr/ppermute | solution.py:17
  232.8 26.9 %collective-permute-start.1 = (bf16[2,256,256]{2,1,0:T(8,128)(2,1)}, bf16[2,256,256]{2,1,0:T(8,128)(2,1)S(1)}, u32[]{:S(2)}, u32[]{:S(2)}) collective-permute-start(bf16[2,256,256]{2,1,0:T(8,128)(2,1)} %get-tuple-element.694), channel_id=1, source_target_pairs={{32,0},{64,32},{96,64},{128,96},{160,128},{192,160},{224,192},{33,... | collective-permute-start | bytes 786440 | tf_op jit(solution)/shard_map/while/body/eval_jaxpr/ppermute | solution.py:17
  259.6 33.5 %collective-permute-start = (bf16[2,256,256]{2,1,0:T(8,128)(2,1)S(1)}, bf16[2,256,256]{2,1,0:T(8,128)(2,1)}, u32[]{:S(2)}, u32[]{:S(2)}) collective-permute-start(bf16[2,256,256]{2,1,0:T(8,128)(2,1)S(1)} %get-tuple-element.764), channel_id=1, source_target_pairs={{0,32},{32,64},{64,96},{96,128},{128,160},{160,192},{192,224},{1,3... | collective-permute-start | bytes 786440 | tf_op jit(solution)/shard_map/while/body/eval_jaxpr/ppermute | solution.py:17
  290.1 8.5 %collective-permute-start.1 = (bf16[2,256,256]{2,1,0:T(8,128)(2,1)}, bf16[2,256,256]{2,1,0:T(8,128)(2,1)S(1)}, u32[]{:S(2)}, u32[]{:S(2)}) collective-permute-start(bf16[2,256,256]{2,1,0:T(8,128)(2,1)} %get-tuple-element.694), channel_id=1, source_target_pairs={{32,0},{64,32},{96,64},{128,96},{160,128},{192,160},{224,192},{33,... | collective-permute-start | bytes 786440 | tf_op jit(solution)/shard_map/while/body/eval_jaxpr/ppermute | solution.py:17
  298.6 26.5 %collective-permute-start = (bf16[2,256,256]{2,1,0:T(8,128)(2,1)S(1)}, bf16[2,256,256]{2,1,0:T(8,128)(2,1)}, u32[]{:S(2)}, u32[]{:S(2)}) collective-permute-start(bf16[2,256,256]{2,1,0:T(8,128)(2,1)S(1)} %get-tuple-element.764), channel_id=1, source_target_pairs={{0,32},{32,64},{64,96},{96,128},{128,160},{160,192},{192,224},{1,3... | collective-permute-start | bytes 786440 | tf_op jit(solution)/shard_map/while/body/eval_jaxpr/ppermute | solution.py:17
  322.1 16.3 %collective-permute-start.1 = (bf16[2,256,256]{2,1,0:T(8,128)(2,1)}, bf16[2,256,256]{2,1,0:T(8,128)(2,1)S(1)}, u32[]{:S(2)}, u32[]{:S(2)}) collective-permute-start(bf16[2,256,256]{2,1,0:T(8,128)(2,1)} %get-tuple-element.694), channel_id=1, source_target_pairs={{32,0},{64,32},{96,64},{128,96},{160,128},{192,160},{224,192},{33,... | collective-permute-start | bytes 786440 | tf_op jit(solution)/shard_map/while/body/eval_jaxpr/ppermute | solution.py:17
  338.4 28.4 %collective-permute-start = (bf16[2,256,256]{2,1,0:T(8,128)(2,1)S(1)}, bf16[2,256,256]{2,1,0:T(8,128)(2,1)}, u32[]{:S(2)}, u32[]{:S(2)}) collective-permute-start(bf16[2,256,256]{2,1,0:T(8,128)(2,1)S(1)} %get-tuple-element.764), channel_id=1, source_target_pairs={{0,32},{32,64},{64,96},{96,128},{128,160},{160,192},{192,224},{1,3... | collective-permute-start | bytes 786440 | tf_op jit(solution)/shard_map/while/body/eval_jaxpr/ppermute | solution.py:17
  363.7 8.7 %collective-permute-start.1 = (bf16[2,256,256]{2,1,0:T(8,128)(2,1)}, bf16[2,256,256]{2,1,0:T(8,128)(2,1)S(1)}, u32[]{:S(2)}, u32[]{:S(2)}) collective-permute-start(bf16[2,256,256]{2,1,0:T(8,128)(2,1)} %get-tuple-element.694), channel_id=1, source_target_pairs={{32,0},{64,32},{96,64},{128,96},{160,128},{192,160},{224,192},{33,... | collective-permute-start | bytes 786440 | tf_op jit(solution)/shard_map/while/body/eval_jaxpr/ppermute | solution.py:17
  372.4 28.4 %collective-permute-start = (bf16[2,256,256]{2,1,0:T(8,128)(2,1)S(1)}, bf16[2,256,256]{2,1,0:T(8,128)(2,1)}, u32[]{:S(2)}, u32[]{:S(2)}) collective-permute-start(bf16[2,256,256]{2,1,0:T(8,128)(2,1)S(1)} %get-tuple-element.764), channel_id=1, source_target_pairs={{0,32},{32,64},{64,96},{96,128},{128,160},{160,192},{192,224},{1,3... | collective-permute-start | bytes 786440 | tf_op jit(solution)/shard_map/while/body/eval_jaxpr/ppermute | solution.py:17
  397.8 13.5 %collective-permute-start.1 = (bf16[2,256,256]{2,1,0:T(8,128)(2,1)}, bf16[2,256,256]{2,1,0:T(8,128)(2,1)S(1)}, u32[]{:S(2)}, u32[]{:S(2)}) collective-permute-start(bf16[2,256,256]{2,1,0:T(8,128)(2,1)} %get-tuple-element.694), channel_id=1, source_target_pairs={{32,0},{64,32},{96,64},{128,96},{160,128},{192,160},{224,192},{33,... | collective-permute-start | bytes 786440 | tf_op jit(solution)/shard_map/while/body/eval_jaxpr/ppermute | solution.py:17
  412.6 12.3 %collective-permute-start.3 = (bf16[1,2,256,512]{3,2,1,0:T(8,128)(2,1)S(1)}, bf16[1,2,256,512]{3,2,1,0:T(8,128)(2,1)S(1)}, u32[]{:S(2)}, u32[]{:S(2)}) collective-permute-start(bf16[1,2,256,512]{3,2,1,0:T(8,128)(2,1)S(1)} %slice.254), channel_id=1, source_target_pairs={{0,1},{1,2},{2,3},{3,4},{4,5},{5,6},{6,7},{7,8},{8,9},{9,10},{10,1... | collective-permute-start | bytes 1572872 | tf_op jit(solution)/shard_map/ppermute | solution.py:11
where the time goes:
time: 429 us; the launch traced here: 427 us
  waiting for transfers between devices  146 us (34%)
  starting transfers between devices  128 us (30%)
  local copies, waits for them, and re-layouts  53.1 us (12%)
  other arithmetic  52.8 us (12%)
  loops' own time  29.5 us (7%)
  matrix products  16.7 us (4%)
    ppermute x22, waiting for transfers between devices, shifted_2(): return lax.ppermute(block, axis, route)  134 us
    ppermute x22, starting transfers between devices, shifted_2(): return lax.ppermute(block, axis, route)  123 us
    dynamic_update_slice x4, local copies, waits for them, and re-layouts, run_behind(): return (adjoint, lax.dynamic_update_slice(gradient, summed, corner))  25.4 us
    another operation x11, loops' own time, advance(): ahead_out = lax.cond(ahead_live, run_ahead, lambda: empty_wave)  15.3 us
    dot_general x24, matrix products, transform(): jnp.einsum('bjk,abkl->ajl', left, table, preferred_element_type=jnp.float32)  15.3 us
    another operation x11, loops' own time, advance(): lax.cond(behind_live, run_behind, lambda: (empty_wave, gradient))  13.9 us
    another operation x11, other arithmetic  13.8 us
    ppermute x2, waiting for transfers between devices, from_behind(): lax.ppermute(x, axis, [(i, (i + by) % devices) for i in range(devices)])  12.2 us
  transfers between devices with their start and end apart: 24, of which 15 were waited for; matrix products, arithmetic and copies ran while one was open for 22% of the time, Pallas kernels for 0%

commit v1 on v0

v1 whole, which is shorter than its diff:
```python
import jax
import jax.numpy as jnp
import numpy as np
from jax import lax
from jax.experimental import pallas as pl
from jax.experimental.pallas import tpu as pltpu
from jax.sharding import PartitionSpec as P


def fit(function, degrees, limit):
    points = limit * np.cos((np.arange(400) + 0.5) * np.pi / 400)
    basis = np.stack([points**degree for degree in degrees], 1)
    return np.linalg.lstsq(basis, function(points), rcond=None)[0]


SIN = [float(value) for value in fit(np.sin, (1, 3, 5, 7, 9), 1.571)]
COS = [float(value) for value in fit(np.cos, (0, 2, 4, 6, 8, 10), 1.571)]


def horner(coefficients, x):
    total = coefficients[-1]
    for value in coefficients[-2::-1]:
        total = total * x + value
    return total


def cis(phase):
    half = phase * 0.5
    square = half * half
    sine = horner(SIN, square) * half
    cosine = horner(COS, square)
    double = sine + sine
    return 1.0 - double * sine, double * cosine


def tables(npix):
    counter = np.arange(npix)
    angles = 2.0 * np.pi / npix * (counter[:, None] * counter[None, :] % npix)
    real_part = (np.cos(angles) / np.sqrt(npix)).astype(np.float32)
    imag_part = (-np.sin(angles) / np.sqrt(npix)).astype(np.float32)
    left = np.block([[real_part, -imag_part], [imag_part, real_part]])
    right = np.block([[real_part, imag_part], [-imag_part, real_part]])
    return jnp.asarray(left, jnp.bfloat16), jnp.asarray(right, jnp.bfloat16)


def dot(first, second):
    return jnp.dot(first, second, preferred_element_type=jnp.float32)


def transform(real, imag, left, right):
    npix = real.shape[0]
    half = dot(left, jnp.concatenate([real, imag], 0)).astype(jnp.bfloat16)
    full = dot(jnp.concatenate([half[:npix], half[npix:]], 1), right)
    return full[:, :npix], full[:, npix:]


def times(a, b, c, d):
    return a * c - b * d, a * d + b * c


def conj_times(a, b, c, d):
    return a * c + b * d, a * d - b * c


def narrow(pair):
    return pair[0].astype(jnp.bfloat16), pair[1].astype(jnp.bfloat16)


def wide(pair):
    return pair[0].astype(jnp.float32), pair[1].astype(jnp.float32)


def cut_kernel(positions, tile, edge, out, extended):
    rows, columns = tile.shape
    npix = out.shape[-1]
    extended[:rows] = tile[...].astype(jnp.float32)
    extended[rows:] = edge[...].astype(jnp.float32)

    def step(index, carry):
        direction, probe = index // 4, index % 4
        row = positions[direction, probe, 0]
        column = positions[direction, probe, 1]
        start = pl.multiple_of(row // 8 * 8, 8)
        strip = extended[pl.ds(start, npix + 8), :]
        strip = pltpu.roll(strip, lax.rem(columns - column, columns), 1)[:, :npix]
        strip = pltpu.roll(strip, lax.rem(npix + 8 - lax.rem(row, 8), npix + 8), 0)
        out[index] = strip[:npix].astype(out.dtype)
        return carry

    lax.fori_loop(0, 8, step, 0)


def chain_kernel(
    place, windows, probe, stored, sent_0, sent_1, sent_2, measured, propagator, left, right, out, shift, wave
):
    device = place[0]
    layers = windows.shape[0]
    shift[0], shift[1] = cis(propagator[...])

    def forward(pair):
        return transform(*pair, left[...], right[...])

    def inverse(pair):
        return transform(*pair, right[...], left[...])

    def advance(pair, layer):
        transmit = cis(windows[layer].astype(jnp.float32))
        exited = narrow(times(*wide(pair), *transmit))
        moved = narrow(times(shift[0], shift[1], *forward(exited)))
        return narrow(inverse(moved))

    @pl.when(device < 4)
    def _():
        wave[...] = probe[...]

        def step(layer, carry):
            pair = advance((wave[0], wave[1]), layer)
            wave[0], wave[1] = pair
            out[layer, 0], out[layer, 1] = pair
            return carry

        lax.fori_loop(0, layers, step, 0)

    @pl.when(device >= 4)
    def _():
        for index, sent in enumerate((sent_0, sent_1, sent_2)):

            @pl.when(device == 4 + index)
            def _():
                wave[...] = sent[...]

        @pl.when(device == 7)
        def _():
            wave[...] = stored[0, 3]

        exit_wave = advance((wave[0], wave[1]), layers - 1)
        real, imag = forward(exit_wave)
        weight = real * real + imag * imag - measured[device - 4]
        wave[0], wave[1] = narrow(inverse(narrow((weight * real, weight * imag))))

        def step(index, carry):
            layer = layers - 1 - index
            moved = narrow(conj_times(shift[0], shift[1], *forward((wave[0], wave[1]))))
            exited = inverse(moved)
            out[layer, 0], out[layer, 1] = narrow(exited)
            transmit = cis(windows[layer].astype(jnp.float32))
            wave[0], wave[1] = narrow(conj_times(*transmit, *exited))
            return carry

        lax.fori_loop(0, layers, step, 0)


def place_kernel(positions, back, stored, leaving, own, rim, total):
    rows, columns = own.shape[1:]
    npix = back.shape[-1]
    leaving[0] = back[:4]
    total[...] = jnp.zeros_like(total)

    def step(probe, carry):
        row = positions[1, probe, 0]
        column = positions[1, probe, 1]
        start = pl.multiple_of(row // 8 * 8, 8)
        pair = conj_times(
            stored[0, probe, 0].astype(jnp.float32),
            stored[0, probe, 1].astype(jnp.float32),
            back[4 + probe, 0].astype(jnp.float32),
            back[4 + probe, 1].astype(jnp.float32),
        )
        for part in range(2):
            padded = jnp.concatenate([pair[part], jnp.zeros((8, npix), jnp.float32)], 0)
            padded = pltpu.roll(padded, lax.rem(row, 8), 0)
            padded = jnp.concatenate([padded, jnp.zeros_like(padded)], 1)
            total[part, pl.ds(start, npix + 8), :] += pltpu.roll(padded, column, 1)
        return carry

    lax.fori_loop(0, 4, step, 0)
    own[...] = total[:, :rows]
    rim[...] = total[:, rows:].astype(rim.dtype)


VMEM = pl.BlockSpec(memory_space=pltpu.VMEM)
SMEM = pl.BlockSpec(memory_space=pltpu.SMEM)
PARAMS = pltpu.CompilerParams(vmem_limit_bytes=40 << 20)


def body(probe, positions, object_phase, propagator, stored, measured):
    npix = probe.shape[-1]
    _, rows, columns = object_phase.shape
    tiles = lax.axis_size("lat")
    depth = lax.axis_size("depth")
    left, right = tables(npix)
    tile = object_phase[0]
    edge = lax.ppermute(tile, "lat", [(i, (i - 1) % tiles) for i in range(tiles)])
    sent = [lax.ppermute(stored[0, i], "depth", [(depth - 1, 4 + i)]) for i in range(3)]
    windows = pl.pallas_call(
        cut_kernel,
        out_shape=jax.ShapeDtypeStruct((8, npix, npix), jnp.bfloat16),
        in_specs=[SMEM, VMEM, VMEM],
        out_specs=VMEM,
        scratch_shapes=[pltpu.VMEM((rows + npix, columns), jnp.float32)],
        compiler_params=PARAMS,
        name="cut",
    )(positions, tile, edge)
    windows = lax.all_to_all(windows, "depth", 0, 0, tiled=True)
    place = lax.axis_index("depth").astype(jnp.int32).reshape(1)
    results = pl.pallas_call(
        chain_kernel,
        out_shape=jax.ShapeDtypeStruct((depth, 2, npix, npix), jnp.bfloat16),
        in_specs=[SMEM] + [VMEM] * 10,
        out_specs=VMEM,
        scratch_shapes=[pltpu.VMEM((2, npix, npix), jnp.float32), pltpu.VMEM((2, npix, npix), jnp.bfloat16)],
        compiler_params=PARAMS,
        name="chain",
    )(place, windows, probe, stored, *sent, measured, propagator, left, right)
    back = lax.all_to_all(results, "depth", 0, 0, tiled=True)
    leaving, own, rim = pl.pallas_call(
        place_kernel,
        out_shape=(
            jax.ShapeDtypeStruct((1, 4, 2, npix, npix), jnp.bfloat16),
            jax.ShapeDtypeStruct((2, rows, columns), jnp.float32),
            jax.ShapeDtypeStruct((2, npix, columns), jnp.bfloat16),
        ),
        in_specs=[SMEM, VMEM, VMEM],
        out_specs=(VMEM, VMEM, VMEM),
        scratch_shapes=[pltpu.VMEM((2, rows + npix, columns), jnp.float32)],
        compiler_params=PARAMS,
        name="place",
    )(positions, back, stored)
    rim = lax.ppermute(rim, "lat", [(i, (i + 1) % tiles) for i in range(tiles)])
    gradient = own + rim.astype(jnp.float32)
    return leaving, gradient[None]


def solution(mesh):
    return jax.shard_map(
        body,
        mesh=mesh,
        in_specs=(
            P(),
            P(None, "lat", None),
            P("depth", "lat", None),
            P(),
            P("depth", "lat", None, None, None),
            P("lat", None, None),
        ),
        out_specs=(P("depth", "lat", None, None, None), P("depth", None, "lat", None)),
        check_vma=False,
    )
```

time: 429 us -> 108 us (0.25)
  waiting for transfers between devices: 146 us -> 24.3 us
  starting transfers between devices: 128 us -> 15.3 us
  other arithmetic: 52.8 us -> 1.13 us
  local copies, waits for them, and re-layouts: 53.1 us -> 5.66 us
  blocking collectives: 0 us -> 37.3 us
  loops' own time: 29.5 us -> 0 us
  Pallas kernels: 0 us -> 21.7 us
  matrix products: 16.7 us -> 0 us
    ppermute x24 -> x5, waiting for transfers between devices: 146 us -> 17.5 us  [the longest x1 14 us: body(): rim = lax.ppermute(rim, 'lat', [(i, (i + 1) % tiles) for i in range(tiles)])]
    ppermute x24 -> x5, starting transfers between devices: 128 us -> 9.27 us  [the longest x1 5.15 us: body(): lax.ppermute(tile, 'lat', [(i, (i - 1) % tiles) for i in range(tiles)])]
    all_to_all x0 -> x1, blocking collectives: none -> 37.3 us  [body(): back = lax.all_to_all(results, 'depth', 0, 0, tiled=True)]
    another operation x27 -> x0, loops' own time: 29.5 us -> none  [the longest x11 15.3 us: advance(): ahead_out = lax.cond(ahead_live, run_ahead, lambda: empty_wave)]
    dynamic_update_slice x4 -> x0, local copies, waits for them, and re-layouts: 25.4 us -> none  [run_behind(): return (adjoint, lax.dynamic_update_slice(gradient, summed, corner))]
    pallas_call x0 -> x3, Pallas kernels: none -> 21.7 us  [the longest x1 14 us: body(): pl.pallas_call(chain_kernel, out_shape=jax.ShapeDtypeStruct((depth, 2, np...]
    another operation x30 -> x0, other arithmetic: 19.3 us -> none
    dot_general x28 -> x0, matrix products: 16.7 us -> none  [the longest x24 15.3 us: transform(): jnp.einsum('bjk,abkl->ajl', left, table, preferred_element_type=jnp.float32)]
  transfers between devices with their start and end apart: 24 -> 6, of which waited for: 15 -> 3; matrix products, arithmetic and copies ran while one was open for 22% -> 2% of each run, Pallas kernels for 0% -> 0%
where the time goes in v1:
time: 108 us; the launch traced here: 106 us
  blocking collectives  37.3 us (35%)
  waiting for transfers between devices  24.3 us (22%)
  Pallas kernels  21.7 us (20%)
  starting transfers between devices  15.3 us (14%)
  local copies, waits for them, and re-layouts  5.66 us (5%)
  other arithmetic  1.13 us (1%)
    all_to_all x1, blocking collectives, body(): back = lax.all_to_all(results, 'depth', 0, 0, tiled=True)  37.3 us
    ppermute x1, waiting for transfers between devices, body(): rim = lax.ppermute(rim, 'lat', [(i, (i + 1) % tiles) for i in range(tiles)])  14 us
    pallas_call x1, Pallas kernels, body(): pl.pallas_call(chain_kernel, out_shape=jax.ShapeDtypeStruct((depth, 2, np...  14 us
    all_to_all x1, waiting for transfers between devices, body(): windows = lax.all_to_all(windows, 'depth', 0, 0, tiled=True)  6.84 us
    all_to_all x1, starting transfers between devices, body(): windows = lax.all_to_all(windows, 'depth', 0, 0, tiled=True)  6.05 us
    ppermute x1, starting transfers between devices, body(): lax.ppermute(tile, 'lat', [(i, (i - 1) % tiles) for i in range(tiles)])  5.15 us
    unnamed x15, local copies, waits for them, and re-layouts  4.77 us
    ppermute x3, starting transfers between devices, body(): lax.ppermute(stored[0, i], 'depth', [(depth - 1, 4 + i)])  4.12 us
  transfers between devices with their start and end apart: 6, of which 3 were waited for; matrix products, arithmetic and copies ran while one was open for 2% of the time, Pallas kernels for 0%

profile of v1, /device:TPU:16, one launch (start us, length us, event | category | flops | bytes accessed | tf_op | source)
XLA Modules:
  0.0 106.1 jit_solution(701138673632872145)
XLA Ops:
  0.6 0.0 copy-start
  0.6 5.1 %collective-permute-start = (bf16[256,512]{1,0:T(8,128)(2,1)}, bf16[256,512]{1,0:T(8,128)(2,1)S(1)}, u32[]{:S(2)}, u32[]{:S(2)}) collective-permute-start(bf16[256,512]{1,0:T(8,128)(2,1)} %bitcast.10), channel_id=1, source_target_pairs={{0,31},{1,0},{2,1},{3,2},{4,3},{5,4},{6,5},{7,6},{8,7},{9,8},{10,9... | collective-permute-start | bytes 786440 | tf_op jit(solution)/shard_map/ppermute | solution.py:193
  5.8 0.8 copy.11.positions
  6.6 3.4 %collective-permute-done.edge = bf16[256,512]{1,0:T(8,128)(2,1)S(1)} collective-permute-done((bf16[256,512]{1,0:T(8,128)(2,1)}, bf16[256,512]{1,0:T(8,128)(2,1)S(1)}, u32[]{:S(2)}, u32[]{:S(2)}) %collective-permute-start) | collective-permute-done | bytes 262176 | tf_op jit(solution)/shard_map/ppermute | solution.py:193
  10.0 0.0 copy-start.6
  10.0 0.9 copy-done.6
  10.9 3.9 %cut.1 = bf16[8,256,256]{2,1,0:T(8,128)(2,1)} custom-call(s32[2,4,2]{2,1,0:T(4,128)S(1)} %copy.11.positions, bf16[256,512]{1,0:T(8,128)(2,1)S(1)} %bitcast.11, bf16[256,512]{1,0:T(8,128)(2,1)S(1)} %collective-permute-done.edge), custom_call_target="tpu_custom_call" | custom-call | tf_op jit(solution)/shard_map/cut/pallas_call | solution.py:195
  14.8 0.0 copy-start.1
  14.8 0.0 copy-start.4
  14.8 6.0 %all-to-all-start = ((bf16[8,256,256]{2,1,0:T(8,128)(2,1)}), bf16[8,256,256]{2,1,0:T(8,128)(2,1)S(1)}, u32[]{:S(2)}, u32[]{:S(2)}) async-start(bf16[8,256,256]{2,1,0:T(8,128)(2,1)} %cut.1), calls=%async_computation | async-start | bytes 2097152 | tf_op jit(solution)/shard_map/all_to_all | solution.py:204
  20.9 0.0 copy-done
  20.9 0.9 slice_bitcast_fusion
  21.8 1.4 %collective-permute-start.3 = (bf16[2,256,256]{2,1,0:T(8,128)(2,1)}, bf16[2,256,256]{2,1,0:T(8,128)(2,1)}, u32[]{:S(2)}, u32[]{:S(2)}) collective-permute-start(bf16[2,256,256]{2,1,0:T(8,128)(2,1)} %get-tuple-element.8), channel_id=1, source_target_pairs={{224,192},{225,193},{226,194},{227,195},{228,196},{229,197},{230,1... | collective-permute-start | bytes 786440 | tf_op jit(solution)/shard_map/ppermute | solution.py:194
  23.2 1.4 %collective-permute-start.2 = (bf16[2,256,256]{2,1,0:T(8,128)(2,1)}, bf16[2,256,256]{2,1,0:T(8,128)(2,1)}, u32[]{:S(2)}, u32[]{:S(2)}) collective-permute-start(bf16[2,256,256]{2,1,0:T(8,128)(2,1)} %get-tuple-element.9), channel_id=1, source_target_pairs={{224,160},{225,161},{226,162},{227,163},{228,164},{229,165},{230,1... | collective-permute-start | bytes 786440 | tf_op jit(solution)/shard_map/ppermute | solution.py:194
  24.5 1.4 %collective-permute-start.1 = (bf16[2,256,256]{2,1,0:T(8,128)(2,1)}, bf16[2,256,256]{2,1,0:T(8,128)(2,1)}, u32[]{:S(2)}, u32[]{:S(2)}) collective-permute-start(bf16[2,256,256]{2,1,0:T(8,128)(2,1)} %get-tuple-element.10), channel_id=1, source_target_pairs={{224,128},{225,129},{226,130},{227,131},{228,132},{229,133},{230,1... | collective-permute-start | bytes 786440 | tf_op jit(solution)/shard_map/ppermute | solution.py:194
  25.9 0.0 collective-permute-done.3.sent_2
  25.9 0.0 collective-permute-done.2.sent_1
  25.9 0.0 collective-permute-done.1.sent_0
  25.9 6.8 %all-to-all-done.windows = bf16[8,256,256]{2,1,0:T(8,128)(2,1)S(1)} async-done(((bf16[8,256,256]{2,1,0:T(8,128)(2,1)}), bf16[8,256,256]{2,1,0:T(8,128)(2,1)S(1)}, u32[]{:S(2)}, u32[]{:S(2)}) %all-to-all-start) | async-done | bytes 1048608 | tf_op jit(solution)/shard_map/all_to_all | solution.py:204
  32.8 0.0 copy-done.1
  32.8 0.0 copy-done.4
  32.8 0.0 copy-start.2
  32.8 1.0 copy-done.2
  33.8 0.0 copy-start.3
  33.8 1.0 copy-done.3
  34.9 0.0 copy-start.5
  34.9 0.9 copy-done.5
  35.8 14.0 %chain.1 = bf16[8,2,256,256]{3,2,1,0:T(8,128)(2,1)S(1)} custom-call(s32[1]{0:T(128)} %bitcast.place, bf16[8,256,256]{2,1,0:T(8,128)(2,1)S(1)} %all-to-all-done.windows, bf16[2,256,256]{2,1,0:T(8,128)(2,1)S(1)} %copy-done.4, bf16[1,4,2,256,256]{4,3,2,1,0:T(8,128)(2,1)S(1)} %copy-done, bf16[2,256,256]{2,1,0:T(8,128)(2,1)} %collective-permute-done.1.sent_0, ...), custom_call_target="tpu_custom_call" | custom-call | tf_op jit(solution)/shard_map/chain/pallas_call | solution.py:206
  49.8 37.3 %all_to_all.10.back = bf16[8,2,256,256]{3,2,1,0:T(8,128)(2,1)S(1)} all-to-all(bf16[8,2,256,256]{3,2,1,0:T(8,128)(2,1)S(1)} %chain.1), channel_id=1, replica_groups=mesh['depth'=8,'lat'=32] {'depth'}, dimensions={0} | all-to-all | bytes 4194304 | tf_op jit(solution)/shard_map/all_to_all | solution.py:215
  87.1 3.9 %place.1 = (bf16[1,4,2,256,256]{4,3,2,1,0:T(8,128)(2,1)}, f32[2,256,512]{2,1,0:T(8,128)S(1)}, bf16[2,256,512]{2,1,0:T(8,128)(2,1)S(1)}) custom-call(s32[2,4,2]{2,1,0:T(4,128)S(1)} %copy.11.positions, bf16[8,2,256,256]{3,2,1,0:T(8,128)(2,1)S(1)} %all_to_all.10.back, bf16[1,4,2,256,256]{4,3,2,1,0:T(8,128)(2,1)S(1)} %copy-done), custom_call_target="tpu_custom_call" | custom-call | tf_op jit(solution)/shard_map/place/pallas_call | solution.py:216
  90.9 0.0 collective-permute-start.4
  91.0 14.0 %collective-permute-done.4 = bf16[2,256,512]{2,1,0:T(8,128)(2,1)S(1)} collective-permute-done((bf16[2,256,512]{2,1,0:T(8,128)(2,1)S(1)}, bf16[2,256,512]{2,1,0:T(8,128)(2,1)S(1)}, u32[]{:S(2)}, u32[]{:S(2)}) %collective-permute-start.4) | collective-permute-done | bytes 524320 | tf_op jit(solution)/shard_map/ppermute | solution.py:229
  105.0 1.1 %add_bitcast_fusion = f32[1,2,256,512]{3,2,1,0:T(8,128)} fusion(f32[2,256,512]{2,1,0:T(8,128)S(1)} %get-tuple-element.6, bf16[2,256,512]{2,1,0:T(8,128)(2,1)S(1)} %collective-permute-done.4), kind=kLoop, calls=%fused_computation | loop fusion | flops 524288 | bytes 2621440 | tf_op jit(solution)/shard_map/broadcast_in_dim | solution.py:231
Async XLA Ops:
  0.6 20.3 %copy-start = (bf16[1,4,2,256,256]{4,3,2,1,0:T(8,128)(2,1)S(1)}, bf16[1,4,2,256,256]{4,3,2,1,0:T(8,128)(2,1)}, u32[]{:S(2)}) copy-start(bf16[1,4,2,256,256]{4,3,2,1,0:T(8,128)(2,1)} %stored.3) | copy-start | bytes 3145732
  0.6 9.4 %collective-permute-start = (bf16[256,512]{1,0:T(8,128)(2,1)}, bf16[256,512]{1,0:T(8,128)(2,1)S(1)}, u32[]{:S(2)}, u32[]{:S(2)}) collective-permute-start(bf16[256,512]{1,0:T(8,128)(2,1)} %bitcast.10), channel_id=1, source_target_pairs={{0,31},{1,0},{2,1},{3,2},{4,3},{5,4},{6,5},{7,6},{8,7},{9,8},{10,9... | collective-permute-start | bytes 786440 | tf_op jit(solution)/shard_map/ppermute | solution.py:193
  10.0 0.9 copy-start.6
  14.8 17.9 %copy-start.1 = (f32[4,256,256]{2,1,0:T(8,128)S(1)}, f32[4,256,256]{2,1,0:T(8,128)}, u32[]{:S(2)}) copy-start(f32[4,256,256]{2,1,0:T(8,128)} %measured.1) | copy-start | bytes 3145732
  14.8 17.9 %copy-start.4 = (bf16[2,256,256]{2,1,0:T(8,128)(2,1)S(1)}, bf16[2,256,256]{2,1,0:T(8,128)(2,1)}, u32[]{:S(2)}) copy-start(bf16[2,256,256]{2,1,0:T(8,128)(2,1)} %probe.1) | copy-start | bytes 786436
  14.8 17.9 %all-to-all-start = ((bf16[8,256,256]{2,1,0:T(8,128)(2,1)}), bf16[8,256,256]{2,1,0:T(8,128)(2,1)S(1)}, u32[]{:S(2)}, u32[]{:S(2)}) async-start(bf16[8,256,256]{2,1,0:T(8,128)(2,1)} %cut.1), calls=%async_computation | async-start | bytes 2097152 | tf_op jit(solution)/shard_map/all_to_all | solution.py:204
  21.8 4.1 %collective-permute-start.3 = (bf16[2,256,256]{2,1,0:T(8,128)(2,1)}, bf16[2,256,256]{2,1,0:T(8,128)(2,1)}, u32[]{:S(2)}, u32[]{:S(2)}) collective-permute-start(bf16[2,256,256]{2,1,0:T(8,128)(2,1)} %get-tuple-element.8), channel_id=1, source_target_pairs={{224,192},{225,193},{226,194},{227,195},{228,196},{229,197},{230,1... | collective-permute-start | bytes 786440 | tf_op jit(solution)/shard_map/ppermute | solution.py:194
  23.2 2.8 %collective-permute-start.2 = (bf16[2,256,256]{2,1,0:T(8,128)(2,1)}, bf16[2,256,256]{2,1,0:T(8,128)(2,1)}, u32[]{:S(2)}, u32[]{:S(2)}) collective-permute-start(bf16[2,256,256]{2,1,0:T(8,128)(2,1)} %get-tuple-element.9), channel_id=1, source_target_pairs={{224,160},{225,161},{226,162},{227,163},{228,164},{229,165},{230,1... | collective-permute-start | bytes 786440 | tf_op jit(solution)/shard_map/ppermute | solution.py:194
  24.5 1.4 %collective-permute-start.1 = (bf16[2,256,256]{2,1,0:T(8,128)(2,1)}, bf16[2,256,256]{2,1,0:T(8,128)(2,1)}, u32[]{:S(2)}, u32[]{:S(2)}) collective-permute-start(bf16[2,256,256]{2,1,0:T(8,128)(2,1)} %get-tuple-element.10), channel_id=1, source_target_pairs={{224,128},{225,129},{226,130},{227,131},{228,132},{229,133},{230,1... | collective-permute-start | bytes 786440 | tf_op jit(solution)/shard_map/ppermute | solution.py:194
  32.8 1.0 copy-start.2
  33.8 1.0 copy-start.3
  34.9 0.9 copy-start.5
  90.9 14.0 %collective-permute-start.4 = (bf16[2,256,512]{2,1,0:T(8,128)(2,1)S(1)}, bf16[2,256,512]{2,1,0:T(8,128)(2,1)S(1)}, u32[]{:S(2)}, u32[]{:S(2)}) collective-permute-start(bf16[2,256,512]{2,1,0:T(8,128)(2,1)S(1)} %get-tuple-element.7), channel_id=1, source_target_pairs={{0,1},{1,2},{2,3},{3,4},{4,5},{5,6},{6,7},{7,8},{8,9},{9,10},{10,1... | collective-permute-start | bytes 1572872 | tf_op jit(solution)/shard_map/ppermute | solution.py:229
